TPU v7x, 32 devices: a whole 2x2x4 slice. The times are simulated.
32 devices in a mesh: row: 8 (over y, x, core), col: 4 (over z).
Axes of the slice: x: 2, y: 2, z: 4, core: 2. Of those that a mesh axis runs over, the one named last changes fastest.
Arguments:
- features: bfloat16 [512, 128, 128], P('row', 'col'), may hold values from -6 to 6
- cotangent: bfloat16 [512, 128, 128], P('row', 'col'), may hold values from -6 to 6
- kernels: bfloat16 [2, 9, 128, 128], replicated, may hold values from -0.1875 to 0.1875
- momentum: float32 [2, 147456], replicated, may hold values from -6 to 6
- mlp_in_weight: float32 [32, 3], replicated, may hold values from -3.5 to 3.5
- mlp_in_bias: float32 [32], replicated, may hold values from -3 to 3
- mlp_out_weight: float32 [2, 32], replicated, may hold values from -1 to 1
- mlp_out_bias: float32 [2], replicated, may hold values from -3 to 3
Outputs:
- update: float32 [2, 147456], replicated
- momentum_out: float32 [2, 147456], replicated
All inputs are finite; a program needn't handle non-finite values.
Results may differ from a plain program's by a relative error of at most 0.0014.
Values may be sent and summed in bfloat16 or wider, within the bound.
A program may use at most 64 MiB of HBM per device.

v0:
```python
import math
import jax
import jax.numpy as jnp
from jax import lax
from jax.sharding import PartitionSpec as P


def padded_2(cells, sides, width):
    for axis, dim in sides:
        count = lax.axis_size(axis)
        head = lax.slice_in_dim(cells, 0, width, axis=dim)
        tail = lax.slice_in_dim(cells, cells.shape[dim] - width, cells.shape[dim], axis=dim)
        cells = jnp.concatenate(
            [
                lax.ppermute(tail, axis, [(i, (i + 1) % count) for i in range(count)]),
                cells,
                lax.ppermute(head, axis, [((i + 1) % count, i) for i in range(count)]),
            ],
            axis=dim,
        )
    return cells


def convolve(padded, kernel, tile_rows, tile_cols):
    channels = padded.shape[-1]
    summed = jnp.zeros((tile_rows * tile_cols, kernel.shape[-1]), jnp.float32)
    for tap_row in range(3):
        for tap_col in range(3):
            window = padded[tap_row : tap_row + tile_rows, tap_col : tap_col + tile_cols].reshape(
                tile_rows * tile_cols, channels
            )
            summed = summed + jnp.dot(
                window, kernel[3 * tap_row + tap_col], preferred_element_type=jnp.float32
            )
    return summed.reshape(tile_rows, tile_cols, -1)


def kernel_grad(padded, cotangent, tile_rows, tile_cols):
    channels = padded.shape[-1]
    flat_cot = cotangent.reshape(tile_rows * tile_cols, -1)
    taps = []
    for tap_row in range(3):
        for tap_col in range(3):
            window = padded[tap_row : tap_row + tile_rows, tap_col : tap_col + tile_cols].reshape(
                tile_rows * tile_cols, channels
            )
            taps.append(
                lax.dot_general(
                    window, flat_cot, (((0,), (0,)), ((), ())), preferred_element_type=jnp.float32
                )
            )
    return jnp.stack(taps)


def transpose_conv(cot_pad, kernel, tile_rows, tile_cols):
    channels = cot_pad.shape[-1]
    summed = jnp.zeros((tile_rows * tile_cols, kernel.shape[-2]), jnp.float32)
    for tap_row in range(3):
        for tap_col in range(3):
            window = cot_pad[
                2 - tap_row : 2 - tap_row + tile_rows, 2 - tap_col : 2 - tap_col + tile_cols
            ].reshape(tile_rows * tile_cols, channels)
            summed = summed + lax.dot_general(
                window,
                kernel[3 * tap_row + tap_col],
                (((1,), (1,)), ((), ())),
                preferred_element_type=jnp.float32,
            )
    return summed.reshape(tile_rows, tile_cols, -1)


def learned_step(grads, squares, momentum, weights, w_in, b_in, w_out, b_out, gain, count):
    norm_scale = 1.0 / jnp.sqrt(squares / count + 1e-06)
    g_hat = grads * norm_scale[:, None]
    momentum_new = 0.9 * momentum + 0.1 * g_hat
    scaled = weights.astype(jnp.float32) * gain
    pre_units = (
        w_in[:, 0][:, None, None] * g_hat[None] + w_in[:, 1][:, None, None] * momentum_new[None]
    )
    pre_units = pre_units + w_in[:, 2][:, None, None] * scaled[None] + b_in[:, None, None]
    units = jax.nn.silu(pre_units)
    mlp_result = (
        jnp.einsum("kh,hlp->klp", w_out, units, precision=lax.Precision.HIGHEST)
        + b_out[:, None, None]
    )
    update = mlp_result[0] * jnp.exp(jnp.tanh(mlp_result[1]))
    return (update, momentum_new)


def on_device(
    features, cotangent, kernels, momentum, mlp_in_weight, mlp_in_bias, mlp_out_weight, mlp_out_bias
):
    tile_rows, tile_cols, channels = features.shape
    param_count = 9 * channels * channels
    image_pad = padded_2(features, (("row", 0), ("col", 1)), 1)
    pre_act = convolve(image_pad, kernels[0], tile_rows, tile_cols)
    hidden = jax.nn.silu(pre_act).astype(jnp.bfloat16)
    hidden_pad = padded_2(hidden, (("row", 0), ("col", 1)), 1)
    cot_pad = padded_2(cotangent, (("row", 0), ("col", 1)), 1)
    grad_two = kernel_grad(hidden_pad, cotangent, tile_rows, tile_cols)
    back_grad = transpose_conv(cot_pad, kernels[1], tile_rows, tile_cols)
    sigma_val = jax.nn.sigmoid(pre_act)
    pre_grad = (back_grad * sigma_val * (1.0 + pre_act * (1.0 - sigma_val))).astype(jnp.bfloat16)
    grad_one = kernel_grad(image_pad, pre_grad, tile_rows, tile_cols)
    local_grads = jnp.stack([grad_one.reshape(-1), grad_two.reshape(-1)])
    weights = kernels.reshape(2, param_count)
    gain = math.sqrt(9.0 * channels)
    grads = lax.psum(local_grads, ("row", "col"))
    squares = jnp.sum(grads * grads, axis=1)
    update, momentum_out = learned_step(
        grads,
        squares,
        momentum,
        weights,
        mlp_in_weight,
        mlp_in_bias,
        mlp_out_weight,
        mlp_out_bias,
        gain,
        float(param_count),
    )
    return (update, momentum_out)


def solution(mesh):
    placed = (P("row", "col", None), P("row", "col", None), P(), P(), P(), P(), P(), P())
    return jax.shard_map(
        on_device, mesh=mesh, in_specs=placed, out_specs=(P(), P()), check_vma=False
    )
```

profile of v0, /device:TPU:0, one launch (start us, length us, event | category | flops | bytes accessed | tf_op | source)
XLA Modules:
  0.0 238.4 jit_solution(3576847353787842551)
XLA Ops:
  7.2 1.3 copy.30
  8.6 0.5 collective-permute-start
  9.1 2.9 %collective-permute-start.1 = (bf16[1,32,128]{2,0,1:T(2,128)(2,1)S(1)}, bf16[1,32,128]{2,0,1:T(2,128)(2,1)S(1)}, u32[]{:S(2)}, u32[]{:S(2)}) collective-permute-start(bf16[1,32,128]{2,0,1:T(2,128)(2,1)S(1)} %get-tuple-element.41), channel_id=1, source_target_pairs={{4,0},{8,4},{12,8},{16,12},{20,16},{24,20},{28,24},{0,28},{5,1},{9... | collective-permute-start | bytes 24584 | tf_op jit(solution)/shard_map/ppermute | solution.py:17
  12.1 0.7 fusion.119
  12.8 2.6 %collective-permute-start.4 = (bf16[1,32,128]{2,1,0:T(8,128)(2,1)S(1)}, bf16[1,32,128]{2,1,0:T(8,128)(2,1)S(1)}, u32[]{:S(2)}, u32[]{:S(2)}) collective-permute-start(bf16[1,32,128]{2,1,0:T(8,128)(2,1)S(1)} %get-tuple-element.34), channel_id=1, source_target_pairs={{4,0},{8,4},{12,8},{16,12},{20,16},{24,20},{28,24},{0,28},{5,1},{9... | collective-permute-start | bytes 24584 | tf_op jit(solution)/shard_map/ppermute | solution.py:17
  15.5 2.3 collective-permute-start.2
  17.8 2.1 collective-permute-start.7
  20.8 0.4 pad_maximum_fusion.7
  21.2 0.3 copy.35
  21.5 0.3 copy.41
  21.9 2.0 collective-permute-start.5
  23.9 0.5 collective-permute-start.6
  24.4 0.3 pad_maximum_fusion.1
  24.8 0.6 fusion.116
  25.4 0.3 copy.33
  26.0 0.3 copy.36
  26.4 0.3 copy.37
  27.8 2.3 collective-permute-done.6
  30.1 0.7 pad_maximum_fusion.11
  32.0 0.7 copy-done.4
  35.7 0.4 fusion.21
  36.0 1.4 fusion.43
  38.5 0.3 fusion.38
  38.8 0.4 fusion.37
  39.2 0.3 fusion.36
  39.6 0.3 fusion.35
  40.1 2.6 %collective-permute-start.9 = (bf16[1,32,128]{2,0,1:T(2,128)(2,1)S(1)}, bf16[1,32,128]{2,0,1:T(2,128)(2,1)S(1)}, u32[]{:S(2)}, u32[]{:S(2)}) collective-permute-start(bf16[1,32,128]{2,0,1:T(2,128)(2,1)S(1)} %get-tuple-element.37), channel_id=1, source_target_pairs={{4,0},{8,4},{12,8},{16,12},{20,16},{24,20},{28,24},{0,28},{5,1},{9... | collective-permute-start | bytes 24584 | tf_op jit(solution)/shard_map/ppermute | solution.py:17
  43.0 1.2 collective-permute-done.8
  44.3 4.0 %collective-permute-start.11 = (bf16[66,1,128]{2,0,1:T(8,128)(2,1)S(1)}, bf16[66,1,128]{2,0,1:T(8,128)(2,1)S(1)}, u32[]{:S(2)}, u32[]{:S(2)}) collective-permute-start(bf16[66,1,128]{2,0,1:T(8,128)(2,1)S(1)} %get-tuple-element.20), channel_id=1, source_target_pairs={{1,0},{2,1},{3,2},{0,3},{5,4},{6,5},{7,6},{4,7},{9,8},{10,9},{11,1... | collective-permute-start | bytes 50696 | tf_op jit(solution)/shard_map/ppermute | solution.py:17
  48.6 1.2 collective-permute-done.10
  49.8 0.4 pad_maximum_fusion.2
  50.2 0.4 fusion.32
  50.6 0.5 fusion.31
  51.1 0.4 fusion.30
  51.4 0.4 fusion.29
  51.9 0.4 fusion.28
  52.3 0.4 fusion.27
  52.7 0.4 fusion.26
  53.2 0.5 fusion.25
  53.7 0.4 fusion.24
  54.1 1.9 pad_maximum_fusion
  56.2 4.3 %copy.91 = f32[1,2,1152,128]{3,1,2,0:T(2,128)S(1)} copy(f32[1,2,1152,128]{3,2,1,0:T(8,128)S(1)} %bitcast.218) | data formatting | bytes 2359296
  60.5 127.9 %all-reduce.2.cloned.1.call-done = f32[2,147456]{1,0:T(2,128)} async-done(((f32[2,147456]{1,0:T(2,128)}), f32[2,147456]{1,0:T(2,128)}) %all-reduce.2.cloned.1.call-update) | async-done | bytes 1179664 | tf_op jit(solution)/shard_map/psum | solution.py:108
  188.4 2.5 %multiply_reduce_fusion = f32[2]{0:T(128)S(1)} fusion(f32[2,147456]{1,0:T(2,128)} %all-reduce.2.cloned.1.call-done), kind=kLoop, calls=%fused_computation.45 | loop fusion | flops 589822 | bytes 1179656 | tf_op jit(solution)/shard_map/reduce_sum | solution.py:109
  191.0 1.3 multiply_add_fusion
  192.4 33.7 %fusion = f32[2,2,147456]{2,0,1:T(2,128)S(1)} fusion(f32[32]{0:T(128)S(1)} %copy-done.8, f32[2,147456]{1,0:T(2,128)S(1)} %bitcast.239, f32[32]{0:T(128)S(1)} %get-tuple-element.43, f32[2,147456]{1,0:T(2,128)S(1)} %get-tuple-element.2, f32[32]{0:T(128)S(1)} %get-tuple-element.44, f32[2,147456]{1,0:T(2,128)S(1)} %get-tuple-element.3, ...), kind=kOutput, calls=%fused_computation.1 | convolution fusion | flops 321454080 | bytes 5899016 | tf_op jit(solution)/shard_map/kh,hlp->klp/dot_general | solution.py:83
  226.1 2.5 %fusion.23 = f32[1,2,147456]{2,0,1:T(1,128)S(1)} fusion(f32[2,2,147456]{2,0,1:T(2,128)S(1)} %fusion), kind=kLoop, calls=%fused_computation.40 | loop fusion | flops 294912 | bytes 3538944 | tf_op jit(solution)/shard_map/mul | solution.py:86
  228.6 2.7 %copy.92 = f32[1,2,147456]{2,1,0:T(2,128)} copy(f32[1,2,147456]{2,0,1:T(1,128)S(1)} %fusion.23) | data formatting | bytes 2359296
  (69 shorter events, 8.4 us)
Async XLA Ops:
  7.2 185.2 %copy-start = (f32[2,32]{1,0:T(2,128)S(1)}, f32[2,32]{1,0:T(2,128)}, u32[]{:S(2)}) copy-start(f32[2,32]{1,0:T(2,128)} %param.14) | copy-start | bytes 772
  7.2 12.7 %copy-start.3 = (bf16[64,32,128]{2,1,0:T(8,128)(2,1)S(1)}, bf16[64,32,128]{2,1,0:T(8,128)(2,1)}, u32[]{:S(2)}) copy-start(bf16[64,32,128]{2,1,0:T(8,128)(2,1)} %param.9) | copy-start | bytes 1572868
  7.2 181.2 %all-reduce.2.cloned.1.call-start = ((), (), s32[]{:S(2)}) async-start(), calls=%async_computation | async-start | bytes 2359296 | tf_op jit(solution)/shard_map/psum | solution.py:108
  8.6 6.8 %collective-permute-start = (bf16[1,32,128]{2,0,1:T(2,128)(2,1)S(1)}, bf16[1,32,128]{2,0,1:T(2,128)(2,1)S(1)}, u32[]{:S(2)}, u32[]{:S(2)}) collective-permute-start(bf16[1,32,128]{2,0,1:T(2,128)(2,1)S(1)} %get-tuple-element.40), channel_id=1, source_target_pairs={{0,4},{4,8},{8,12},{12,16},{16,20},{20,24},{24,28},{28,0},{1,5},{5... | collective-permute-start | bytes 24584 | tf_op jit(solution)/shard_map/ppermute | solution.py:15
  9.1 6.3 %collective-permute-start.1 = (bf16[1,32,128]{2,0,1:T(2,128)(2,1)S(1)}, bf16[1,32,128]{2,0,1:T(2,128)(2,1)S(1)}, u32[]{:S(2)}, u32[]{:S(2)}) collective-permute-start(bf16[1,32,128]{2,0,1:T(2,128)(2,1)S(1)} %get-tuple-element.41), channel_id=1, source_target_pairs={{4,0},{8,4},{12,8},{16,12},{20,16},{24,20},{28,24},{0,28},{5,1},{9... | collective-permute-start | bytes 24584 | tf_op jit(solution)/shard_map/ppermute | solution.py:17
  12.8 7.1 %collective-permute-start.3 = (bf16[1,32,128]{2,1,0:T(8,128)(2,1)S(1)}, bf16[1,32,128]{2,1,0:T(8,128)(2,1)S(1)}, u32[]{:S(2)}, u32[]{:S(2)}) collective-permute-start(bf16[1,32,128]{2,1,0:T(8,128)(2,1)S(1)} %get-tuple-element.35), channel_id=1, source_target_pairs={{0,4},{4,8},{8,12},{12,16},{16,20},{20,24},{24,28},{28,0},{1,5},{5... | collective-permute-start | bytes 24584 | tf_op jit(solution)/shard_map/ppermute | solution.py:15
  12.8 7.1 %collective-permute-start.4 = (bf16[1,32,128]{2,1,0:T(8,128)(2,1)S(1)}, bf16[1,32,128]{2,1,0:T(8,128)(2,1)S(1)}, u32[]{:S(2)}, u32[]{:S(2)}) collective-permute-start(bf16[1,32,128]{2,1,0:T(8,128)(2,1)S(1)} %get-tuple-element.34), channel_id=1, source_target_pairs={{4,0},{8,4},{12,8},{16,12},{20,16},{24,20},{28,24},{0,28},{5,1},{9... | collective-permute-start | bytes 24584 | tf_op jit(solution)/shard_map/ppermute | solution.py:17
  15.4 4.8 %copy-start.2 = (bf16[2,9,128,128]{3,2,1,0:T(8,128)(2,1)S(1)}, bf16[2,9,128,128]{3,2,1,0:T(8,128)(2,1)}, u32[]{:S(2)}) copy-start(bf16[2,9,128,128]{3,2,1,0:T(8,128)(2,1)} %param.10) | copy-start | bytes 1769476
  15.5 9.0 %collective-permute-start.2 = (bf16[66,1,128]{2,0,1:T(8,128)(2,1)S(1)}, bf16[66,1,128]{2,0,1:T(8,128)(2,1)S(1)}, u32[]{:S(2)}, u32[]{:S(2)}) collective-permute-start(bf16[66,1,128]{2,0,1:T(8,128)(2,1)S(1)} %get-tuple-element.25), channel_id=1, source_target_pairs={{0,1},{1,2},{2,3},{3,0},{4,5},{5,6},{6,7},{7,4},{8,9},{9,10},{10,1... | collective-permute-start | bytes 50696 | tf_op jit(solution)/shard_map/ppermute | solution.py:15
  17.8 6.6 %collective-permute-start.7 = (bf16[66,1,128]{2,0,1:T(8,128)(2,1)S(1)}, bf16[66,1,128]{2,0,1:T(8,128)(2,1)S(1)}, u32[]{:S(2)}, u32[]{:S(2)}) collective-permute-start(bf16[66,1,128]{2,0,1:T(8,128)(2,1)S(1)} %get-tuple-element.24), channel_id=1, source_target_pairs={{1,0},{2,1},{3,2},{0,3},{5,4},{6,5},{7,6},{4,7},{9,8},{10,9},{11,1... | collective-permute-start | bytes 50696 | tf_op jit(solution)/shard_map/ppermute | solution.py:17
  21.9 5.9 %collective-permute-start.5 = (bf16[66,1,128]{2,1,0:T(2,128)(2,1)S(1)}, bf16[66,1,128]{2,1,0:T(2,128)(2,1)S(1)}, u32[]{:S(2)}, u32[]{:S(2)}) collective-permute-start(bf16[66,1,128]{2,1,0:T(2,128)(2,1)S(1)} %get-tuple-element.29), channel_id=1, source_target_pairs={{1,0},{2,1},{3,2},{0,3},{5,4},{6,5},{7,6},{4,7},{9,8},{10,9},{11,1... | collective-permute-start | bytes 50696 | tf_op jit(solution)/shard_map/ppermute | solution.py:17
  23.9 6.2 %collective-permute-start.6 = (bf16[66,1,128]{2,1,0:T(2,128)(2,1)S(1)}, bf16[66,1,128]{2,1,0:T(2,128)(2,1)S(1)}, u32[]{:S(2)}, u32[]{:S(2)}) collective-permute-start(bf16[66,1,128]{2,1,0:T(2,128)(2,1)S(1)} %get-tuple-element.30), channel_id=1, source_target_pairs={{0,1},{1,2},{2,3},{3,0},{4,5},{5,6},{6,7},{7,4},{8,9},{9,10},{10,1... | collective-permute-start | bytes 50696 | tf_op jit(solution)/shard_map/ppermute | solution.py:15
  31.7 1.0 copy-start.4
  40.0 4.2 %collective-permute-start.8 = (bf16[1,32,128]{2,0,1:T(2,128)(2,1)S(1)}, bf16[1,32,128]{2,0,1:T(2,128)(2,1)S(1)}, u32[]{:S(2)}, u32[]{:S(2)}) collective-permute-start(bf16[1,32,128]{2,0,1:T(2,128)(2,1)S(1)} %get-tuple-element.36), channel_id=1, source_target_pairs={{0,4},{4,8},{8,12},{12,16},{16,20},{20,24},{24,28},{28,0},{1,5},{5... | collective-permute-start | bytes 24584 | tf_op jit(solution)/shard_map/ppermute | solution.py:15
  40.1 4.1 %collective-permute-start.9 = (bf16[1,32,128]{2,0,1:T(2,128)(2,1)S(1)}, bf16[1,32,128]{2,0,1:T(2,128)(2,1)S(1)}, u32[]{:S(2)}, u32[]{:S(2)}) collective-permute-start(bf16[1,32,128]{2,0,1:T(2,128)(2,1)S(1)} %get-tuple-element.37), channel_id=1, source_target_pairs={{4,0},{8,4},{12,8},{16,12},{20,16},{24,20},{28,24},{0,28},{5,1},{9... | collective-permute-start | bytes 24584 | tf_op jit(solution)/shard_map/ppermute | solution.py:17
  44.2 5.6 %collective-permute-start.10 = (bf16[66,1,128]{2,0,1:T(8,128)(2,1)S(1)}, bf16[66,1,128]{2,0,1:T(8,128)(2,1)S(1)}, u32[]{:S(2)}, u32[]{:S(2)}) collective-permute-start(bf16[66,1,128]{2,0,1:T(8,128)(2,1)S(1)} %get-tuple-element.21), channel_id=1, source_target_pairs={{0,1},{1,2},{2,3},{3,0},{4,5},{5,6},{6,7},{7,4},{8,9},{9,10},{10,1... | collective-permute-start | bytes 50696 | tf_op jit(solution)/shard_map/ppermute | solution.py:15
  44.3 5.5 %collective-permute-start.11 = (bf16[66,1,128]{2,0,1:T(8,128)(2,1)S(1)}, bf16[66,1,128]{2,0,1:T(8,128)(2,1)S(1)}, u32[]{:S(2)}, u32[]{:S(2)}) collective-permute-start(bf16[66,1,128]{2,0,1:T(8,128)(2,1)S(1)} %get-tuple-element.20), channel_id=1, source_target_pairs={{1,0},{2,1},{3,2},{0,3},{5,4},{6,5},{7,6},{4,7},{9,8},{10,9},{11,1... | collective-permute-start | bytes 50696 | tf_op jit(solution)/shard_map/ppermute | solution.py:17
  56.2 4.3 %copy-start.7 = (f32[32,3]{0,1:T(4,128)S(1)}, f32[32,3]{0,1:T(4,128)}, u32[]{:S(2)}) copy-start(f32[32,3]{0,1:T(4,128)} %param.12) | copy-start | bytes 1156
  56.2 134.7 %copy-start.5 = (f32[2,147456]{1,0:T(2,128)S(1)}, f32[2,147456]{1,0:T(2,128)}, u32[]{:S(2)}) copy-start(f32[2,147456]{1,0:T(2,128)} %param.11) | copy-start | bytes 3538948
  188.4 2.5 %copy-start.1 = (f32[2,147456]{1,0:T(2,128)S(1)}, f32[2,147456]{1,0:T(2,128)}, u32[]{:S(2)}) copy-start(f32[2,147456]{1,0:T(2,128)} %all-reduce.2.cloned.1.call-done) | copy-start | bytes 3538948
  190.9 1.4 copy-start.8
  191.0 1.4 copy-start.9
  192.3 33.8 %copy-start.6 = (f32[2,147456]{1,0:T(2,128)}, f32[2,147456]{1,0:T(2,128)S(1)}, u32[]{:S(2)}) copy-start(f32[2,147456]{1,0:T(2,128)S(1)} %get-tuple-element.2) | copy-start | bytes 3538948
Sparse Core Ops, SparseCore 0:
  56.2 132.2 all-reduce.1
where the time goes:
time: 241 us; the launch traced here: 238 us
  waiting for transfers between devices  133 us (55%)
  matrix products  46 us (19%)
  starting transfers between devices  19.8 us (8%)
  between operations  14.8 us (6%)
  local copies, waits for them, and re-layouts  13.3 us (6%)
  other arithmetic  11.9 us (5%)
    psum x1, waiting for transfers between devices, on_device(): grads = lax.psum(local_grads, ('row', 'col'))  128 us
    dot_general x1, matrix products, learned_step(): jnp.einsum('kh,hlp->klp', w_out, units, precision=lax.Precision.HIGHEST)  33.7 us
    ppermute x6, starting transfers between devices, padded_2(): lax.ppermute(head, axis, [((i + 1) % count, i) for i in range(count)])  16.3 us
    unnamed x24, local copies, waits for them, and re-layouts  9.07 us
    dot_general x18, matrix products, kernel_grad(): lax.dot_general(window, flat_cot, (((0,), (0,)), ((), ())), preferred_ele...  7.03 us
  transfers between devices with their start and end apart: 13, of which 4 were waited for; matrix products, arithmetic and copies ran while one was open for 5% of the time, Pallas kernels for 0%

commit v1 on v0

--- a/solution.py
+++ b/solution.py
@@ -105,7 +105,7 @@
     local_grads = jnp.stack([grad_one.reshape(-1), grad_two.reshape(-1)])
     weights = kernels.reshape(2, param_count)
     gain = math.sqrt(9.0 * channels)
-    grads = lax.psum(local_grads, ("row", "col"))
+    grads = lax.psum(lax.psum(local_grads, "row"), "col")
     squares = jnp.sum(grads * grads, axis=1)
     update, momentum_out = learned_step(
         grads,

time: 241 us -> 225 us (0.934)
  waiting for transfers between devices: 133 us -> 115 us
    psum x1 -> x2, waiting for transfers between devices: 128 us -> 110 us  [on_device(): grads = lax.psum(lax.psum(local_grads, 'row'), 'col')]
    unnamed x24 -> x26, local copies, waits for them, and re-layouts: 9.07 us -> 9.88 us
  transfers between devices with their start and end apart: 13 -> 14, of which waited for: 4 -> 5; matrix products, arithmetic and copies ran while one was open for 5% -> 5% of each run, Pallas kernels for 0% -> 0%
where the time goes in v1:
time: 225 us; the launch traced here: 222 us
  waiting for transfers between devices  115 us (51%)
  matrix products  46 us (20%)
  starting transfers between devices  19.8 us (9%)
  between operations  14.8 us (7%)
  local copies, waits for them, and re-layouts  14.2 us (6%)
  other arithmetic  11.9 us (5%)
    psum x2, waiting for transfers between devices, on_device(): grads = lax.psum(lax.psum(local_grads, 'row'), 'col')  110 us
    dot_general x1, matrix products, learned_step(): jnp.einsum('kh,hlp->klp', w_out, units, precision=lax.Precision.HIGHEST)  33.7 us
    ppermute x6, starting transfers between devices, padded_2(): lax.ppermute(head, axis, [((i + 1) % count, i) for i in range(count)])  16.3 us
    unnamed x26, local copies, waits for them, and re-layouts  9.88 us
    dot_general x18, matrix products, kernel_grad(): lax.dot_general(window, flat_cot, (((0,), (0,)), ((), ())), preferred_ele...  7.02 us
    ppermute x6, waiting for transfers between devices, padded_2(): lax.ppermute(tail, axis, [(i, (i + 1) % count) for i in range(count)])  4.59 us
  transfers between devices with their start and end apart: 14, of which 5 were waited for; matrix products, arithmetic and copies ran while one was open for 5% of the time, Pallas kernels for 0%

profile of v1, /device:TPU:0, one launch (start us, length us, event | category | flops | bytes accessed | tf_op | source)
XLA Modules:
  0.0 221.7 jit_solution(6491871045853965267)
XLA Ops:
  7.2 1.3 copy.30
  8.6 0.5 collective-permute-start
  9.1 2.9 %collective-permute-start.1 = (bf16[1,32,128]{2,0,1:T(2,128)(2,1)S(1)}, bf16[1,32,128]{2,0,1:T(2,128)(2,1)S(1)}, u32[]{:S(2)}, u32[]{:S(2)}) collective-permute-start(bf16[1,32,128]{2,0,1:T(2,128)(2,1)S(1)} %get-tuple-element.41), channel_id=1, source_target_pairs={{4,0},{8,4},{12,8},{16,12},{20,16},{24,20},{28,24},{0,28},{5,1},{9... | collective-permute-start | bytes 24584 | tf_op jit(solution)/shard_map/ppermute | solution.py:17
  12.1 0.7 fusion.119
  12.8 2.6 %collective-permute-start.4 = (bf16[1,32,128]{2,1,0:T(8,128)(2,1)S(1)}, bf16[1,32,128]{2,1,0:T(8,128)(2,1)S(1)}, u32[]{:S(2)}, u32[]{:S(2)}) collective-permute-start(bf16[1,32,128]{2,1,0:T(8,128)(2,1)S(1)} %get-tuple-element.34), channel_id=1, source_target_pairs={{4,0},{8,4},{12,8},{16,12},{20,16},{24,20},{28,24},{0,28},{5,1},{9... | collective-permute-start | bytes 24584 | tf_op jit(solution)/shard_map/ppermute | solution.py:17
  15.5 2.3 %collective-permute-start.2 = (bf16[66,1,128]{2,0,1:T(8,128)(2,1)S(1)}, bf16[66,1,128]{2,0,1:T(8,128)(2,1)S(1)}, u32[]{:S(2)}, u32[]{:S(2)}) collective-permute-start(bf16[66,1,128]{2,0,1:T(8,128)(2,1)S(1)} %get-tuple-element.25), channel_id=1, source_target_pairs={{0,1},{1,2},{2,3},{3,0},{4,5},{5,6},{6,7},{7,4},{8,9},{9,10},{10,1... | collective-permute-start | bytes 50696 | tf_op jit(solution)/shard_map/ppermute | solution.py:15
  17.8 2.1 collective-permute-start.7
  20.9 0.4 pad_maximum_fusion.7
  21.3 0.3 copy.35
  21.6 0.3 copy.41
  22.0 2.0 collective-permute-start.5
  23.9 0.5 collective-permute-start.6
  24.5 0.4 pad_maximum_fusion.1
  24.8 0.7 fusion.116
  25.6 0.3 copy.33
  26.2 0.3 copy.36
  26.5 0.3 copy.37
  27.9 2.2 collective-permute-done.6
  30.1 0.7 pad_maximum_fusion.11
  32.0 0.7 copy-done.4
  35.7 0.4 fusion.21
  36.1 1.4 fusion.43
  37.9 0.4 fusion.40
  38.9 0.4 fusion.37
  40.1 2.6 %collective-permute-start.9 = (bf16[1,32,128]{2,0,1:T(2,128)(2,1)S(1)}, bf16[1,32,128]{2,0,1:T(2,128)(2,1)S(1)}, u32[]{:S(2)}, u32[]{:S(2)}) collective-permute-start(bf16[1,32,128]{2,0,1:T(2,128)(2,1)S(1)} %get-tuple-element.37), channel_id=1, source_target_pairs={{4,0},{8,4},{12,8},{16,12},{20,16},{24,20},{28,24},{0,28},{5,1},{9... | collective-permute-start | bytes 24584 | tf_op jit(solution)/shard_map/ppermute | solution.py:17
  42.7 0.3 fusion.34
  43.1 1.2 collective-permute-done.8
  44.4 4.0 %collective-permute-start.11 = (bf16[66,1,128]{2,0,1:T(8,128)(2,1)S(1)}, bf16[66,1,128]{2,0,1:T(8,128)(2,1)S(1)}, u32[]{:S(2)}, u32[]{:S(2)}) collective-permute-start(bf16[66,1,128]{2,0,1:T(8,128)(2,1)S(1)} %get-tuple-element.20), channel_id=1, source_target_pairs={{1,0},{2,1},{3,2},{0,3},{5,4},{6,5},{7,6},{4,7},{9,8},{10,9},{11,1... | collective-permute-start | bytes 50696 | tf_op jit(solution)/shard_map/ppermute | solution.py:17
  48.7 1.2 collective-permute-done.10
  49.9 0.4 pad_maximum_fusion.2
  50.3 0.4 fusion.32
  50.7 0.5 fusion.31
  51.1 0.4 fusion.30
  51.5 0.5 fusion.29
  52.0 0.4 fusion.28
  52.4 0.4 fusion.27
  52.8 0.4 fusion.26
  53.3 0.5 fusion.25
  53.7 0.4 fusion.24
  54.2 1.9 pad_maximum_fusion
  56.2 57.9 %all-reduce.3.cloned.1.call-done = f32[2,147456]{1,0:T(2,128)} async-done(((f32[2,147456]{1,0:T(2,128)}), f32[2,147456]{1,0:T(2,128)}) %all-reduce.3.cloned.1.call-update) | async-done | bytes 1179664 | tf_op jit(solution)/shard_map/psum | solution.py:108
  114.3 5.1 %copy.91 = f32[1,2,1152,128]{3,1,2,0:T(2,128)} copy(f32[1,2,1152,128]{3,2,1,0:T(8,128)S(1)} %bitcast.218) | data formatting | bytes 2359296
  119.4 52.3 %all-reduce.5.cloned.1.call-done = f32[2,147456]{1,0:T(2,128)} async-done(((f32[2,147456]{1,0:T(2,128)}), f32[2,147456]{1,0:T(2,128)}) %all-reduce.5.cloned.1.call-update) | async-done | bytes 1179664 | tf_op jit(solution)/shard_map/psum | solution.py:108
  171.7 2.5 %multiply_reduce_fusion = f32[2]{0:T(128)S(1)} fusion(f32[2,147456]{1,0:T(2,128)} %all-reduce.5.cloned.1.call-done), kind=kLoop, calls=%fused_computation.45 | loop fusion | flops 589822 | bytes 1179656 | tf_op jit(solution)/shard_map/reduce_sum | solution.py:109
  174.3 1.4 multiply_add_fusion
  175.7 33.7 %fusion = f32[2,2,147456]{2,0,1:T(2,128)S(1)} fusion(f32[32]{0:T(128)S(1)} %copy-done.9, f32[2,147456]{1,0:T(2,128)S(1)} %bitcast.239, f32[32]{0:T(128)S(1)} %get-tuple-element.43, f32[2,147456]{1,0:T(2,128)S(1)} %get-tuple-element.2, f32[32]{0:T(128)S(1)} %get-tuple-element.44, f32[2,147456]{1,0:T(2,128)S(1)} %get-tuple-element.3, ...), kind=kOutput, calls=%fused_computation.1 | convolution fusion | flops 321454080 | bytes 5899016 | tf_op jit(solution)/shard_map/kh,hlp->klp/dot_general | solution.py:83
  209.4 2.5 %fusion.23 = f32[1,2,147456]{2,0,1:T(1,128)S(1)} fusion(f32[2,2,147456]{2,0,1:T(2,128)S(1)} %fusion), kind=kLoop, calls=%fused_computation.40 | loop fusion | flops 294912 | bytes 3538944 | tf_op jit(solution)/shard_map/mul | solution.py:86
  212.0 2.7 %copy.92 = f32[1,2,147456]{2,1,0:T(2,128)} copy(f32[1,2,147456]{2,0,1:T(1,128)S(1)} %fusion.23) | data formatting | bytes 2359296
  (74 shorter events, 8.9 us)
Async XLA Ops:
  7.2 168.5 %copy-start = (f32[2,32]{1,0:T(2,128)S(1)}, f32[2,32]{1,0:T(2,128)}, u32[]{:S(2)}) copy-start(f32[2,32]{1,0:T(2,128)} %param.14) | copy-start | bytes 772
  7.2 12.7 %copy-start.3 = (bf16[64,32,128]{2,1,0:T(8,128)(2,1)S(1)}, bf16[64,32,128]{2,1,0:T(8,128)(2,1)}, u32[]{:S(2)}) copy-start(bf16[64,32,128]{2,1,0:T(8,128)(2,1)} %param.9) | copy-start | bytes 1572868
  7.2 106.9 %all-reduce.3.cloned.1.call-start = ((), (), s32[]{:S(2)}) async-start(), calls=%async_computation | async-start | bytes 2359296 | tf_op jit(solution)/shard_map/psum | solution.py:108
  8.6 6.8 %collective-permute-start = (bf16[1,32,128]{2,0,1:T(2,128)(2,1)S(1)}, bf16[1,32,128]{2,0,1:T(2,128)(2,1)S(1)}, u32[]{:S(2)}, u32[]{:S(2)}) collective-permute-start(bf16[1,32,128]{2,0,1:T(2,128)(2,1)S(1)} %get-tuple-element.40), channel_id=1, source_target_pairs={{0,4},{4,8},{8,12},{12,16},{16,20},{20,24},{24,28},{28,0},{1,5},{5... | collective-permute-start | bytes 24584 | tf_op jit(solution)/shard_map/ppermute | solution.py:15
  9.1 6.3 %collective-permute-start.1 = (bf16[1,32,128]{2,0,1:T(2,128)(2,1)S(1)}, bf16[1,32,128]{2,0,1:T(2,128)(2,1)S(1)}, u32[]{:S(2)}, u32[]{:S(2)}) collective-permute-start(bf16[1,32,128]{2,0,1:T(2,128)(2,1)S(1)} %get-tuple-element.41), channel_id=1, source_target_pairs={{4,0},{8,4},{12,8},{16,12},{20,16},{24,20},{28,24},{0,28},{5,1},{9... | collective-permute-start | bytes 24584 | tf_op jit(solution)/shard_map/ppermute | solution.py:17
  12.8 7.1 %collective-permute-start.3 = (bf16[1,32,128]{2,1,0:T(8,128)(2,1)S(1)}, bf16[1,32,128]{2,1,0:T(8,128)(2,1)S(1)}, u32[]{:S(2)}, u32[]{:S(2)}) collective-permute-start(bf16[1,32,128]{2,1,0:T(8,128)(2,1)S(1)} %get-tuple-element.35), channel_id=1, source_target_pairs={{0,4},{4,8},{8,12},{12,16},{16,20},{20,24},{24,28},{28,0},{1,5},{5... | collective-permute-start | bytes 24584 | tf_op jit(solution)/shard_map/ppermute | solution.py:15
  12.8 7.1 %collective-permute-start.4 = (bf16[1,32,128]{2,1,0:T(8,128)(2,1)S(1)}, bf16[1,32,128]{2,1,0:T(8,128)(2,1)S(1)}, u32[]{:S(2)}, u32[]{:S(2)}) collective-permute-start(bf16[1,32,128]{2,1,0:T(8,128)(2,1)S(1)} %get-tuple-element.34), channel_id=1, source_target_pairs={{4,0},{8,4},{12,8},{16,12},{20,16},{24,20},{28,24},{0,28},{5,1},{9... | collective-permute-start | bytes 24584 | tf_op jit(solution)/shard_map/ppermute | solution.py:17
  15.4 4.8 %copy-start.2 = (bf16[2,9,128,128]{3,2,1,0:T(8,128)(2,1)S(1)}, bf16[2,9,128,128]{3,2,1,0:T(8,128)(2,1)}, u32[]{:S(2)}) copy-start(bf16[2,9,128,128]{3,2,1,0:T(8,128)(2,1)} %param.10) | copy-start | bytes 1769476
  15.5 9.0 %collective-permute-start.2 = (bf16[66,1,128]{2,0,1:T(8,128)(2,1)S(1)}, bf16[66,1,128]{2,0,1:T(8,128)(2,1)S(1)}, u32[]{:S(2)}, u32[]{:S(2)}) collective-permute-start(bf16[66,1,128]{2,0,1:T(8,128)(2,1)S(1)} %get-tuple-element.25), channel_id=1, source_target_pairs={{0,1},{1,2},{2,3},{3,0},{4,5},{5,6},{6,7},{7,4},{8,9},{9,10},{10,1... | collective-permute-start | bytes 50696 | tf_op jit(solution)/shard_map/ppermute | solution.py:15
  17.8 6.7 %collective-permute-start.7 = (bf16[66,1,128]{2,0,1:T(8,128)(2,1)S(1)}, bf16[66,1,128]{2,0,1:T(8,128)(2,1)S(1)}, u32[]{:S(2)}, u32[]{:S(2)}) collective-permute-start(bf16[66,1,128]{2,0,1:T(8,128)(2,1)S(1)} %get-tuple-element.24), channel_id=1, source_target_pairs={{1,0},{2,1},{3,2},{0,3},{5,4},{6,5},{7,6},{4,7},{9,8},{10,9},{11,1... | collective-permute-start | bytes 50696 | tf_op jit(solution)/shard_map/ppermute | solution.py:17
  22.0 6.0 %collective-permute-start.5 = (bf16[66,1,128]{2,1,0:T(2,128)(2,1)S(1)}, bf16[66,1,128]{2,1,0:T(2,128)(2,1)S(1)}, u32[]{:S(2)}, u32[]{:S(2)}) collective-permute-start(bf16[66,1,128]{2,1,0:T(2,128)(2,1)S(1)} %get-tuple-element.29), channel_id=1, source_target_pairs={{1,0},{2,1},{3,2},{0,3},{5,4},{6,5},{7,6},{4,7},{9,8},{10,9},{11,1... | collective-permute-start | bytes 50696 | tf_op jit(solution)/shard_map/ppermute | solution.py:17
  23.9 6.2 %collective-permute-start.6 = (bf16[66,1,128]{2,1,0:T(2,128)(2,1)S(1)}, bf16[66,1,128]{2,1,0:T(2,128)(2,1)S(1)}, u32[]{:S(2)}, u32[]{:S(2)}) collective-permute-start(bf16[66,1,128]{2,1,0:T(2,128)(2,1)S(1)} %get-tuple-element.30), channel_id=1, source_target_pairs={{0,1},{1,2},{2,3},{3,0},{4,5},{5,6},{6,7},{7,4},{8,9},{9,10},{10,1... | collective-permute-start | bytes 50696 | tf_op jit(solution)/shard_map/ppermute | solution.py:15
  31.7 1.0 copy-start.4
  40.0 4.2 %collective-permute-start.8 = (bf16[1,32,128]{2,0,1:T(2,128)(2,1)S(1)}, bf16[1,32,128]{2,0,1:T(2,128)(2,1)S(1)}, u32[]{:S(2)}, u32[]{:S(2)}) collective-permute-start(bf16[1,32,128]{2,0,1:T(2,128)(2,1)S(1)} %get-tuple-element.36), channel_id=1, source_target_pairs={{0,4},{4,8},{8,12},{12,16},{16,20},{20,24},{24,28},{28,0},{1,5},{5... | collective-permute-start | bytes 24584 | tf_op jit(solution)/shard_map/ppermute | solution.py:15
  40.1 4.2 %collective-permute-start.9 = (bf16[1,32,128]{2,0,1:T(2,128)(2,1)S(1)}, bf16[1,32,128]{2,0,1:T(2,128)(2,1)S(1)}, u32[]{:S(2)}, u32[]{:S(2)}) collective-permute-start(bf16[1,32,128]{2,0,1:T(2,128)(2,1)S(1)} %get-tuple-element.37), channel_id=1, source_target_pairs={{4,0},{8,4},{12,8},{16,12},{20,16},{24,20},{28,24},{0,28},{5,1},{9... | collective-permute-start | bytes 24584 | tf_op jit(solution)/shard_map/ppermute | solution.py:17
  44.3 5.6 %collective-permute-start.10 = (bf16[66,1,128]{2,0,1:T(8,128)(2,1)S(1)}, bf16[66,1,128]{2,0,1:T(8,128)(2,1)S(1)}, u32[]{:S(2)}, u32[]{:S(2)}) collective-permute-start(bf16[66,1,128]{2,0,1:T(8,128)(2,1)S(1)} %get-tuple-element.21), channel_id=1, source_target_pairs={{0,1},{1,2},{2,3},{3,0},{4,5},{5,6},{6,7},{7,4},{8,9},{9,10},{10,1... | collective-permute-start | bytes 50696 | tf_op jit(solution)/shard_map/ppermute | solution.py:15
  44.4 5.5 %collective-permute-start.11 = (bf16[66,1,128]{2,0,1:T(8,128)(2,1)S(1)}, bf16[66,1,128]{2,0,1:T(8,128)(2,1)S(1)}, u32[]{:S(2)}, u32[]{:S(2)}) collective-permute-start(bf16[66,1,128]{2,0,1:T(8,128)(2,1)S(1)} %get-tuple-element.20), channel_id=1, source_target_pairs={{1,0},{2,1},{3,2},{0,3},{5,4},{6,5},{7,6},{4,7},{9,8},{10,9},{11,1... | collective-permute-start | bytes 50696 | tf_op jit(solution)/shard_map/ppermute | solution.py:17
  56.1 115.6 %all-reduce.5.cloned.1.call-start = ((), (), s32[]{:S(2)}) async-start(), calls=%async_computation.1 | async-start | bytes 2359296 | tf_op jit(solution)/shard_map/psum | solution.py:108
  114.3 5.1 %copy-start.8 = (f32[32,3]{0,1:T(4,128)S(1)}, f32[32,3]{0,1:T(4,128)}, u32[]{:S(2)}) copy-start(f32[32,3]{0,1:T(4,128)} %param.12) | copy-start | bytes 1156
  114.3 60.0 %copy-start.5 = (f32[2,147456]{1,0:T(2,128)S(1)}, f32[2,147456]{1,0:T(2,128)}, u32[]{:S(2)}) copy-start(f32[2,147456]{1,0:T(2,128)} %param.11) | copy-start | bytes 3538948
  171.7 2.5 %copy-start.1 = (f32[2,147456]{1,0:T(2,128)S(1)}, f32[2,147456]{1,0:T(2,128)}, u32[]{:S(2)}) copy-start(f32[2,147456]{1,0:T(2,128)} %all-reduce.5.cloned.1.call-done) | copy-start | bytes 3538948
  174.3 1.4 copy-start.7
  174.3 1.4 copy-start.9
  174.3 1.4 copy-start.10
  175.7 33.8 %copy-start.6 = (f32[2,147456]{1,0:T(2,128)}, f32[2,147456]{1,0:T(2,128)S(1)}, u32[]{:S(2)}) copy-start(f32[2,147456]{1,0:T(2,128)S(1)} %get-tuple-element.2) | copy-start | bytes 3538948
Sparse Core Ops, SparseCore 0:
  56.2 57.8 all-reduce.2
  116.5 55.2 all-reduce.4
